TPU v7x, 32 devices: a whole 2x2x4 slice. The times are simulated.
32 devices in a mesh: groups: 2 (over x), seq: 8 (over z, y), chan: 2 (over core).
Axes of the slice: x: 2, y: 2, z: 4, core: 2. Of those that a mesh axis runs over, the one named last changes fastest.
Arguments:
- stream: bfloat16 [4096, 2048], P(('groups', 'seq'), 'chan'), parts along dimension 0, may hold values from -6 to 6
- nucleotide_token_ids: int32 [4096], P(('groups', 'seq')), parts along dimension 0, may hold values from 4 to 11, as said below
- genome_length: int32 [2], P('groups'), parts along dimension 0, may hold values from 1024 to 2048
- embedding: bfloat16 [16, 2048], replicated, may hold values from -6 to 6
- attention_in: bfloat16 [2048, 3, 1024], P(None, None, 'chan'), may hold values from -0.125 to 0.125
- scan_input: bfloat16 [2048, 1024], P(None, 'chan'), may hold values from -0.125 to 0.125
- state_maps: bfloat16 [2048, 256], P(None, 'chan'), may hold values from -0.125 to 0.125
- step_weight: bfloat16 [2048, 8], P(None, 'chan'), may hold values from -0.125 to 0.125
- step_bias: float32 [8], P('chan'), may hold values from -1 to 1
- head_decay_speed: float32 [8], P('chan'), as said below
- attention_gain: float32 [1024], P('chan'), may hold values from 0.25 to 1.75
- scan_gain: float32 [1024], P('chan'), may hold values from 0.25 to 1.75
- out_weight: bfloat16 [1024, 2048], P('chan'), may hold values from -0.1875 to 0.1875
Outputs:
- block_out: bfloat16 [4096, 2048], P(('groups', 'seq'), 'chan'), parts along dimension 0
There are 2 independent parts, one for each index of `groups`. A program takes and returns all parts, laid end to end along the dimension named above; an argument that names none is the same for every part. Nothing has to cross between parts.
Inputs may be any that keep to these rules, and one draw needn't show every extreme that they name: `nucleotide_token_ids`: positions below genome_length hold bases 7 to 10, except exactly three positions that hold 11, one in each third of the valid range; positions at or above genome_length hold 4. `head_decay_speed`: every entry lies between 1 / 20480 and 8 / 256.
All inputs are finite; a program needn't handle non-finite values.
Results may differ from a plain program's by a relative error of at most 0.0058.
Values may be sent and summed in bfloat16 or wider, within the bound.
A program may use at most 128 MiB of HBM per device.

v0:
```python
import math
import jax
import jax.numpy as jnp
from jax import lax
from jax.sharding import PartitionSpec as P

HEAD_DIM = 128
STATE = 64
epsilon_norm = 1e-06
spike_logarithm = math.log(0.7)
unclear_nucleotide = 11


def passed_along(block, axis, distance):
    devices = range(lax.axis_size(axis))
    route = [((i - distance) % len(devices), i) for i in devices]
    return lax.ppermute(block, axis, route)


def normalize(values):
    return values * lax.rsqrt(jnp.mean(values * values, axis=-1, keepdims=True) + epsilon_norm)


def compose(earlier_part, later_part):
    return (
        earlier_part[0] * later_part[0],
        later_part[0][:, None, None] * earlier_part[1] + later_part[1],
    )


def key_block(query_tile_rows, key_fragment, value_piece, key_position, valid_limit, score_scale):
    scores = (
        jnp.einsum(
            "epq,fpq->pef", query_tile_rows, key_fragment, preferred_element_type=jnp.float32
        )
        * score_scale
    )
    weights = jnp.where((key_position < valid_limit)[None, None, :], jnp.exp(scores), 0.0)
    totals = jnp.sum(weights, axis=-1).T
    numerator = jnp.einsum(
        "gfa,agn->fgn",
        weights.astype(jnp.bfloat16),
        value_piece,
        preferred_element_type=jnp.float32,
    )
    return (numerator, totals)


def local(
    stream,
    nucleotide_token_ids,
    genome_length,
    embedding,
    attention_in,
    scan_input,
    state_maps,
    step_weight,
    step_bias,
    head_decay_speed,
    attention_gain,
    scan_gain,
    out_weight,
):
    row_count = stream.shape[0]
    model_width = embedding.shape[1]
    head_count = step_weight.shape[1]
    score_scale = 2.0 / math.sqrt(HEAD_DIM)
    valid_limit = genome_length[0]
    position = lax.axis_index("seq") * row_count + jnp.arange(row_count, dtype=jnp.int32)
    key_valid = position < valid_limit
    gathered = lax.all_gather(stream, "chan", axis=1, tiled=True)
    onehot = (
        nucleotide_token_ids[:, None] == jnp.arange(embedding.shape[0], dtype=jnp.int32)[None, :]
    ).astype(jnp.bfloat16)
    hidden = (
        gathered.astype(jnp.float32)
        + jnp.dot(onehot, embedding, preferred_element_type=jnp.float32)
    ).astype(jnp.bfloat16)
    projected = jnp.dot(
        hidden,
        attention_in.reshape(model_width, 3 * head_count * HEAD_DIM),
        preferred_element_type=jnp.float32,
    ).reshape(row_count, 3, head_count, HEAD_DIM)
    queries = normalize(projected[:, 0]).astype(jnp.bfloat16)
    keyset = normalize(projected[:, 1]).astype(jnp.bfloat16)
    valueset = projected[:, 2].astype(jnp.bfloat16)
    empty_numer = jnp.zeros((row_count, head_count, HEAD_DIM), jnp.float32)
    empty_total = jnp.zeros((row_count, head_count), jnp.float32)
    carry_pair = (empty_numer, empty_total)
    key_fragment = lax.all_gather(keyset, "seq", axis=0, tiled=True)
    value_piece = lax.all_gather(valueset, "seq", axis=0, tiled=True)
    piece_rows = key_fragment.shape[0]
    block_count = piece_rows // 512

    def absorb_block(running, element):
        key_block_rows, value_block_rows, first_row = element
        numer_part, total_part = key_block(
            queries,
            key_block_rows,
            value_block_rows,
            first_row + jnp.arange(512, dtype=jnp.int32),
            valid_limit,
            score_scale,
        )
        return ((running[0] + numer_part, running[1] + total_part), None)

    first_rows = 512 * jnp.arange(block_count, dtype=jnp.int32)
    carry_pair, _ = lax.scan(
        absorb_block,
        carry_pair,
        (
            key_fragment.reshape(block_count, 512, head_count, HEAD_DIM),
            value_piece.reshape(block_count, 512, head_count, HEAD_DIM),
            first_rows,
        ),
    )
    numerator, totals = carry_pair
    attended = normalize(numerator / totals[:, :, None])
    inputs = (
        jax.nn.silu(jnp.dot(hidden, scan_input, preferred_element_type=jnp.float32))
        .astype(jnp.bfloat16)
        .reshape(row_count, head_count, HEAD_DIM)
    )
    state_rows = jax.nn.silu(
        jnp.dot(hidden, state_maps, preferred_element_type=jnp.float32)
    ).astype(jnp.bfloat16)
    input_map = state_rows[:, :STATE]
    output_map = state_rows[:, STATE:]
    step_list = jax.nn.softplus(
        jnp.dot(hidden, step_weight, preferred_element_type=jnp.float32) + step_bias[None, :]
    )
    usable_rows = key_valid.astype(jnp.float32)[:, None]
    spike_events = jnp.where(nucleotide_token_ids == unclear_nucleotide, spike_logarithm, 0.0)[
        :, None
    ]
    logarithm_decay = usable_rows * (-head_decay_speed[None, :] * step_list + spike_events)
    used_steps = usable_rows * step_list
    forward = jnp.cumsum(logarithm_decay, axis=0)
    backward = jnp.flip(jnp.cumsum(jnp.flip(logarithm_decay, 0), axis=0), 0)
    inputs_wide = inputs.astype(jnp.float32)
    scaled_forward = (
        (jnp.exp(forward[-1:] - forward) * used_steps)[:, :, None] * inputs_wide
    ).astype(jnp.bfloat16)
    scaled_backward = (
        (jnp.exp(backward[:1] - backward) * used_steps)[:, :, None] * inputs_wide
    ).astype(jnp.bfloat16)
    own_forward = (
        jnp.exp(forward[-1]),
        jnp.einsum("the,ts->hes", scaled_forward, input_map, preferred_element_type=jnp.float32),
    )
    own_backward = (
        jnp.exp(backward[0]),
        jnp.einsum("the,ts->hes", scaled_backward, input_map, preferred_element_type=jnp.float32),
    )
    section_count = lax.axis_size("seq").bit_length() - 1
    distances = [1] + [1 << section for section in range(section_count)]
    window_forward = own_forward
    window_backward = own_backward
    for section_index, distance in enumerate(distances):
        received_up = passed_along((window_forward[0], window_forward[1]), "seq", distance)
        received_down = passed_along((window_backward[0], window_backward[1]), "seq", -distance)
        if section_index == 0:
            window_forward = received_up
            window_backward = received_down
        else:
            window_forward = compose(received_up, window_forward)
            window_backward = compose(received_down, window_backward)
    enter_forward = window_forward[1] / (1.0 - window_forward[0])[:, None, None]
    enter_backward = window_backward[1] / (1.0 - window_backward[0])[:, None, None]
    pairing = jnp.dot(output_map, input_map.T, preferred_element_type=jnp.float32)
    block_rows = jnp.arange(row_count)
    causal_mask = block_rows[:, None] >= block_rows[None, :]
    read_wide = output_map.astype(jnp.float32)

    def strand(cumulative, allowed, entering):
        across = cumulative.T
        exponent = across[:, :, None] - across[:, None, :]
        mixing = (
            pairing[None]
            * jnp.exp(jnp.where(allowed[None], exponent, -jnp.inf))
            * used_steps.T[:, None, :]
        ).astype(jnp.bfloat16)
        local_part = jnp.einsum("htu,uhe->the", mixing, inputs, preferred_element_type=jnp.float32)
        carried = jnp.exp(cumulative)[:, :, None] * jnp.einsum(
            "ts,hes->the", read_wide, entering, precision=lax.Precision.HIGHEST
        )
        return local_part + carried

    scanned = normalize(
        strand(forward, causal_mask, enter_forward)
        + strand(backward, causal_mask.T, enter_backward)
    )
    combined = (
        (
            attention_gain.reshape(head_count, HEAD_DIM) * attended
            + scan_gain.reshape(head_count, HEAD_DIM) * scanned
        )
        .astype(jnp.bfloat16)
        .reshape(row_count, head_count * HEAD_DIM)
    )
    partial_out = jnp.dot(combined, out_weight, preferred_element_type=jnp.float32)
    summed = lax.psum_scatter(partial_out, "chan", scatter_dimension=1, tiled=True)
    return (stream.astype(jnp.float32) + summed).astype(jnp.bfloat16)


def solution(mesh):
    placed = (
        P(("groups", "seq"), "chan"),
        P(("groups", "seq")),
        P("groups"),
        P(),
        P(None, None, "chan"),
        P(None, "chan"),
        P(None, "chan"),
        P(None, "chan"),
        P("chan"),
        P("chan"),
        P("chan"),
        P("chan"),
        P("chan", None),
    )
    return jax.shard_map(
        local, mesh=mesh, in_specs=placed, out_specs=P(("groups", "seq"), "chan"), check_vma=False
    )
```

profile of v0, /device:TPU:0, one launch (start us, length us, event | category | flops | bytes accessed | tf_op | source)
XLA Modules:
  0.0 197.7 jit_solution(5060600774243856370)
XLA Ops:
  7.3 8.9 %copy.26 = bf16[2048,3,512]{0,2,1:T(8,128)(2,1)} copy(bf16[2048,3,512]{2,0,1:T(8,128)(2,1)} %param.19) | data formatting | bytes 12582912 | tf_op args[4]
  16.2 4.4 %all-gather.5.cloned.1.call-done = bf16[256,2048]{1,0:T(8,128)(2,1)} async-done(((bf16[256,1024]{1,0:T(8,128)(2,1)}), bf16[256,2048]{1,0:T(8,128)(2,1)}) %all-gather.5.cloned.1.call-update) | async-done | bytes 1048592 | tf_op jit(solution)/shard_map/all_gather | solution.py:71
  20.7 1.7 fusion.13
  22.4 5.0 %fusion.17 = f32[256,3,4,128]{0,3,2,1:T(8,128)S(1)} fusion(bf16[3,4,128,2048]{3,2,1,0:T(8,128)(2,1)} %bitcast.158, bf16[256,2048]{1,0:T(8,128)(2,1)S(1)} %fusion.13), kind=kOutput, calls=%fused_computation.29 | convolution fusion | flops 1610612736 | bytes 8912896 | tf_op jit(solution)/shard_map/dot_general | solution.py:79
  31.5 1.8 slice.90
  33.2 2.2 %add_multiply_fusion.1 = (f32[4,256]{1,0:T(4,128)S(1)}, f32[4,256]{1,0:T(4,128)}, f32[256,4]{0,1:T(4,128)S(1)}) fusion(f32[256]{0:T(256)S(1)} %compare_select_fusion.2, f32[4]{0:T(128)S(1)} %neg.22, f32[256]{0:T(256)S(1)} %compare_convert_fusion, f32[4]{0:T(128)S(1)} %copy-done.11, bf16[256,2048]{1,0:T(8,128)(2,1)} %copy-done.3, ...), kind=kOutput, calls=%fused_computation.121 | convolution fusion | flops 4205568 | bytes 1079328 | tf_op jit(solution)/shard_map/dot_general | solution.py:130
  37.8 1.7 collective-permute-start
  39.6 1.9 multiply_convert_fusion.7
  41.5 2.7 %fusion.43 = bf16[32,4,8,128]{3,2,1,0:T(8,128)(2,1)S(1)} fusion(bf16[256,2048]{1,0:T(8,128)(2,1)} %copy-done.3, bf16[2048,512]{1,0:T(8,128)(2,1)} %param.20), kind=kOutput, calls=%fused_computation.72 | convolution fusion | flops 537526272 | bytes 3407872 | tf_op jit(solution)/shard_map/dot_general | solution.py:120
  45.2 1.5 collective-permute-start.3
  49.5 3.2 %collective-permute-start.8 = (f32[4]{0:T(128)}, f32[4]{0:T(128)}, u32[]{:S(2)}, u32[]{:S(2)}) collective-permute-start(f32[4]{0:T(128)} %exp.54), channel_id=1, source_target_pairs={{2,0},{4,2},{6,4},{8,6},{10,8},{12,10},{14,12},{0,14},{3,1},{5,3},... | collective-permute-start | bytes 56 | tf_op jit(solution)/shard_map/ppermute | solution.py:17
  54.6 1.5 convolution_bitcast_fusion.2
  56.6 1.7 collective-permute-start.1
  58.4 3.0 %collective-permute-start.9 = (f32[4]{0:T(128)}, f32[4]{0:T(128)S(1)}, u32[]{:S(2)}, u32[]{:S(2)}) collective-permute-start(f32[4]{0:T(128)} %collective-permute-done.8), channel_id=1, source_target_pairs={{2,0},{4,2},{6,4},{8,6},{10,8},{12,10},{14,12},{0,14},{3,1},{5,3},... | collective-permute-start | bytes 56 | tf_op jit(solution)/shard_map/ppermute | solution.py:17
  61.4 1.7 collective-permute-done.1
  64.4 3.8 %collective-permute-start.10 = (f32[4]{0:T(128)S(1)}, f32[4]{0:T(128)S(1)}, u32[]{:S(2)}, u32[]{:S(2)}) collective-permute-start(f32[4]{0:T(128)S(1)} %mul.298), channel_id=1, source_target_pairs={{4,0},{6,2},{8,4},{10,6},{12,8},{14,10},{0,12},{2,14},{5,1},{7,3},... | collective-permute-start | bytes 56 | tf_op jit(solution)/shard_map/ppermute | solution.py:17
  69.5 2.5 %collective-permute-start.15 = (f32[4]{0:T(128)S(1)}, f32[4]{0:T(128)S(1)}, u32[]{:S(2)}, u32[]{:S(2)}) collective-permute-start(f32[4]{0:T(128)S(1)} %mul.299), channel_id=1, source_target_pairs={{8,0},{10,2},{12,4},{14,6},{0,8},{2,10},{4,12},{6,14},{9,1},{11,3}... | collective-permute-start | bytes 56 | tf_op jit(solution)/shard_map/ppermute | solution.py:17
  72.0 1.5 collective-permute-done.7
  74.0 1.7 collective-permute-start.4
  75.7 3.8 %collective-permute-done.12 = f32[4,128,64]{1,2,0:T(8,128)S(1)} collective-permute-done((f32[4,128,64]{1,2,0:T(8,128)S(1)}, f32[4,128,64]{1,2,0:T(8,128)S(1)}, u32[]{:S(2)}, u32[]{:S(2)}) %collective-permute-start.12) | collective-permute-done | bytes 131104 | tf_op jit(solution)/shard_map/ppermute | solution.py:17
  80.2 1.9 collective-permute-start.13
  82.1 3.3 %collective-permute-done.4 = f32[4,128,64]{1,2,0:T(8,128)S(1)} collective-permute-done((f32[4,128,64]{1,2,0:T(8,128)S(1)}, f32[4,128,64]{1,2,0:T(8,128)S(1)}, u32[]{:S(2)}, u32[]{:S(2)}) %collective-permute-start.4) | collective-permute-done | bytes 131104 | tf_op jit(solution)/shard_map/ppermute | solution.py:17
  86.7 7.5 %collective-permute-start.14 = (f32[4,128,64]{1,2,0:T(8,128)S(1)}, f32[4,128,64]{1,2,0:T(8,128)S(1)}, u32[]{:S(2)}, u32[]{:S(2)}) collective-permute-start(f32[4,128,64]{1,2,0:T(8,128)S(1)} %multiply_add_fusion), channel_id=1, source_target_pairs={{8,0},{10,2},{12,4},{14,6},{0,8},{2,10},{4,12},{6,14},{9,1},{11,3}... | collective-permute-start | bytes 393224 | tf_op jit(solution)/shard_map/ppermute | solution.py:17
  94.2 3.7 %collective-permute-done.5 = f32[4,128,64]{1,2,0:T(8,128)S(1)} collective-permute-done((f32[4,128,64]{1,2,0:T(8,128)S(1)}, f32[4,128,64]{1,2,0:T(8,128)S(1)}, u32[]{:S(2)}, u32[]{:S(2)}) %collective-permute-start.5) | collective-permute-done | bytes 131104 | tf_op jit(solution)/shard_map/ppermute | solution.py:17
  98.0 1.3 collective-permute-start.6
  99.3 2.2 %collective-permute-done.14 = f32[4,128,64]{1,2,0:T(8,128)S(1)} collective-permute-done((f32[4,128,64]{1,2,0:T(8,128)S(1)}, f32[4,128,64]{1,2,0:T(8,128)S(1)}, u32[]{:S(2)}, u32[]{:S(2)}) %collective-permute-start.14) | collective-permute-done | bytes 131104 | tf_op jit(solution)/shard_map/ppermute | solution.py:17
  102.0 6.3 %collective-permute-done.6 = f32[4,128,64]{1,2,0:T(8,128)S(1)} collective-permute-done((f32[4,128,64]{1,2,0:T(8,128)S(1)}, f32[4,128,64]{1,2,0:T(8,128)S(1)}, u32[]{:S(2)}, u32[]{:S(2)}) %collective-permute-start.6) | collective-permute-done | bytes 131104 | tf_op jit(solution)/shard_map/ppermute | solution.py:17
  108.8 4.5 %reshape.152 = bf16[4,512,4,128]{1,0,3,2:T(4,128)(2,1)} reshape(bf16[2048,4,128]{0,2,1:T(8,128)(2,1)} %all-gather.7.cloned.1.call-done) | data formatting | bytes 4194304 | tf_op jit(solution)/shard_map/reshape | solution.py:112
  113.3 4.5 %copy.28 = bf16[4,512,4,128]{3,1,2,0:T(8,128)(2,1)} copy(bf16[4,512,4,128]{1,0,3,2:T(4,128)(2,1)} %reshape.152) | data formatting | bytes 4194304
  117.8 24.4 %all-gather.9.cloned.1.call-done = bf16[2048,1,4,128]{0,3,2,1:T(8,128)(2,1)} async-done(((bf16[256,1,4,128]{0,3,2,1:T(8,128)(2,1)}), bf16[2048,1,4,128]{0,3,2,1:T(8,128)(2,1)}) %all-gather.9.cloned.1.call-update) | async-done | bytes 2097168 | tf_op jit(solution)/shard_map/all_gather | solution.py:91
  142.3 4.5 %reshape.151 = bf16[4,512,4,128]{1,0,3,2:T(4,128)(2,1)} reshape(bf16[2048,1,4,128]{0,3,2,1:T(8,128)(2,1)} %all-gather.9.cloned.1.call-done) | data formatting | bytes 4194304 | tf_op jit(solution)/shard_map/reshape | solution.py:113
  146.8 3.4 %copy.27 = bf16[4,512,4,128]{1,3,2,0:T(8,128)(2,1)} copy(bf16[4,512,4,128]{1,0,3,2:T(4,128)(2,1)} %reshape.151) | data formatting | bytes 4194304
  150.1 28.5 %while.13 = (s32[]{:T(128)}, f32[256,4,128]{0,2,1:T(8,128)S(1)}, f32[256,4]{0,1:T(4,128)S(1)}, bf16[4,512,4,128]{1,3,2,0:T(8,128)(2,1)}, s32[4]{0:T(128)S(1)}, /...) while((s32[]{:T(128)}, f32[256,4,128]{0,2,1:T(8,128)S(1)}, ...), condition=%wide.region_4.5_spmd.clone, body=%wide.region_2.4_spmd.clone.sunk | while | flops 271845376 | bytes 6572676 | solution.py:108
  150.7 1.3 add_compare_fusion.2
  152.0 2.9 %bitcast_reduce_fusion.2 = (f32[4,256]{1,0:T(4,128)S(1)}, f32[4,512,256]{2,1,0:T(8,128)}) fusion(pred[512]{0:T(512)(128)(4,1)S(1)} %add_compare_fusion.2, bf16[256,4,128]{2,0,1:T(8,128)(2,1)S(1)} %get-tuple-element.209, bf16[4,512,4,128]{3,1,2,0:T(8,128)(2,1)} %get-tuple-element.208, s32[]{:T(128)} %get-tuple-element.192), kind=kOutput, calls=%fused_computation.clone.1 | convolution fusion | flops 135789568 | bytes 2888704 | tf_op jit(solution)/shard_map/while/body/eval_jaxpr/epq,fpq->pef/dot_general | solution.py:33
  154.9 2.3 %fusion.94 = f32[256,4,128]{0,2,1:T(8,128)S(1)} fusion(f32[4,512,256]{2,1,0:T(8,128)} %get-tuple-element.180, pred[512]{0:T(512)(128)(4,1)S(1)} %add_compare_fusion.2, f32[256,4,128]{0,2,1:T(8,128)S(1)} %get-tuple-element.193, bf16[4,512,4,128]{1,3,2,0:T(8,128)(2,1)} %get-tuple-element.205, s32[]{:T(128)} %get-tuple-element.192, pred[]{:T(512)S(6)} %compare.3), kind=kOutput, calls=%fused_computation.4.clone.1 | convolution fusion | flops 136052736 | bytes 3671041 | tf_op jit(solution)/shard_map/while/body/eval_jaxpr/gfa,agn->fgn/dot_general | solution.py:40
  157.9 1.3 add_compare_fusion.2
  159.2 2.9 %bitcast_reduce_fusion.2 = (f32[4,256]{1,0:T(4,128)S(1)}, f32[4,512,256]{2,1,0:T(8,128)}) fusion(pred[512]{0:T(512)(128)(4,1)S(1)} %add_compare_fusion.2, bf16[256,4,128]{2,0,1:T(8,128)(2,1)S(1)} %get-tuple-element.209, bf16[4,512,4,128]{3,1,2,0:T(8,128)(2,1)} %get-tuple-element.208, s32[]{:T(128)} %get-tuple-element.192), kind=kOutput, calls=%fused_computation.clone.1 | convolution fusion | flops 135789568 | bytes 2888704 | tf_op jit(solution)/shard_map/while/body/eval_jaxpr/epq,fpq->pef/dot_general | solution.py:33
  162.1 2.3 %fusion.94 = f32[256,4,128]{0,2,1:T(8,128)S(1)} fusion(f32[4,512,256]{2,1,0:T(8,128)} %get-tuple-element.180, pred[512]{0:T(512)(128)(4,1)S(1)} %add_compare_fusion.2, f32[256,4,128]{0,2,1:T(8,128)S(1)} %get-tuple-element.193, bf16[4,512,4,128]{1,3,2,0:T(8,128)(2,1)} %get-tuple-element.205, s32[]{:T(128)} %get-tuple-element.192, pred[]{:T(512)S(6)} %compare.3), kind=kOutput, calls=%fused_computation.4.clone.1 | convolution fusion | flops 136052736 | bytes 3671041 | tf_op jit(solution)/shard_map/while/body/eval_jaxpr/gfa,agn->fgn/dot_general | solution.py:40
  165.0 1.3 add_compare_fusion.2
  166.3 2.9 %bitcast_reduce_fusion.2 = (f32[4,256]{1,0:T(4,128)S(1)}, f32[4,512,256]{2,1,0:T(8,128)}) fusion(pred[512]{0:T(512)(128)(4,1)S(1)} %add_compare_fusion.2, bf16[256,4,128]{2,0,1:T(8,128)(2,1)S(1)} %get-tuple-element.209, bf16[4,512,4,128]{3,1,2,0:T(8,128)(2,1)} %get-tuple-element.208, s32[]{:T(128)} %get-tuple-element.192), kind=kOutput, calls=%fused_computation.clone.1 | convolution fusion | flops 135789568 | bytes 2888704 | tf_op jit(solution)/shard_map/while/body/eval_jaxpr/epq,fpq->pef/dot_general | solution.py:33
  169.2 2.3 %fusion.94 = f32[256,4,128]{0,2,1:T(8,128)S(1)} fusion(f32[4,512,256]{2,1,0:T(8,128)} %get-tuple-element.180, pred[512]{0:T(512)(128)(4,1)S(1)} %add_compare_fusion.2, f32[256,4,128]{0,2,1:T(8,128)S(1)} %get-tuple-element.193, bf16[4,512,4,128]{1,3,2,0:T(8,128)(2,1)} %get-tuple-element.205, s32[]{:T(128)} %get-tuple-element.192, pred[]{:T(512)S(6)} %compare.3), kind=kOutput, calls=%fused_computation.4.clone.1 | convolution fusion | flops 136052736 | bytes 3671041 | tf_op jit(solution)/shard_map/while/body/eval_jaxpr/gfa,agn->fgn/dot_general | solution.py:40
  172.1 1.3 add_compare_fusion.2
  173.4 2.9 %bitcast_reduce_fusion.2 = (f32[4,256]{1,0:T(4,128)S(1)}, f32[4,512,256]{2,1,0:T(8,128)}) fusion(pred[512]{0:T(512)(128)(4,1)S(1)} %add_compare_fusion.2, bf16[256,4,128]{2,0,1:T(8,128)(2,1)S(1)} %get-tuple-element.209, bf16[4,512,4,128]{3,1,2,0:T(8,128)(2,1)} %get-tuple-element.208, s32[]{:T(128)} %get-tuple-element.192), kind=kOutput, calls=%fused_computation.clone.1 | convolution fusion | flops 135789568 | bytes 2888704 | tf_op jit(solution)/shard_map/while/body/eval_jaxpr/epq,fpq->pef/dot_general | solution.py:33
  176.3 2.3 %fusion.94 = f32[256,4,128]{0,2,1:T(8,128)S(1)} fusion(f32[4,512,256]{2,1,0:T(8,128)} %get-tuple-element.180, pred[512]{0:T(512)(128)(4,1)S(1)} %add_compare_fusion.2, f32[256,4,128]{0,2,1:T(8,128)S(1)} %get-tuple-element.193, bf16[4,512,4,128]{1,3,2,0:T(8,128)(2,1)} %get-tuple-element.205, s32[]{:T(128)} %get-tuple-element.192, pred[]{:T(512)S(6)} %compare.3), kind=kOutput, calls=%fused_computation.4.clone.1 | convolution fusion | flops 136052736 | bytes 3671041 | tf_op jit(solution)/shard_map/while/body/eval_jaxpr/gfa,agn->fgn/dot_general | solution.py:40
  179.0 2.1 %fusion.77 = f32[256,2048]{1,0:T(8,128)} fusion(bf16[256,512]{0,1:T(8,128)(2,1)S(1)} %bitcast.159, bf16[512,2048]{1,0:T(8,128)(2,1)S(1)} %copy-done), kind=kOutput, calls=%fused_computation.137 | convolution fusion | flops 536870912 | bytes 4456448 | tf_op jit(solution)/shard_map/dot_general | solution.py:201
  181.1 7.9 %reduce-scatter.2.cloned.1.call-done = f32[256,1024]{1,0:T(8,128)} async-done(((f32[256,2048]{1,0:T(8,128)}), f32[256,1024]{1,0:T(8,128)}) %reduce-scatter.2.cloned.1.call-update) | async-done | bytes 1048592 | tf_op jit(solution)/shard_map/reduce_scatter | solution.py:202
  189.0 2.2 %add_convert_fusion = bf16[256,1024]{1,0:T(8,128)(2,1)} fusion(f32[256,1024]{1,0:T(8,128)} %reduce-scatter.2.cloned.1.call-done, bf16[256,1024]{1,0:T(8,128)(2,1)S(1)} %copy-done.2), kind=kLoop, calls=%fused_computation.31 | loop fusion | flops 786432 | bytes 2097152 | tf_op jit(solution)/shard_map/convert_element_type | solution.py:203
  (121 shorter events, 21.5 us)
Async XLA Ops:
  6.5 172.5 %copy-start = (bf16[512,2048]{1,0:T(8,128)(2,1)S(1)}, bf16[512,2048]{1,0:T(8,128)(2,1)}, u32[]{:S(2)}) copy-start(bf16[512,2048]{1,0:T(8,128)(2,1)} %param.27) | copy-start | bytes 6291460
  6.5 14.1 %all-gather.5.cloned.1.call-start = ((), (), s32[]{:S(2)}) async-start(), calls=%async_computation.1 | async-start | bytes 1572864 | tf_op jit(solution)/shard_map/all_gather | solution.py:71
  7.3 13.4 %copy-start.4 = (bf16[16,2048]{1,0:T(8,128)(2,1)S(1)}, bf16[16,2048]{1,0:T(8,128)(2,1)}, u32[]{:S(2)}) copy-start(bf16[16,2048]{1,0:T(8,128)(2,1)} %param.18) | copy-start | bytes 196612
  7.3 13.4 %copy-start.6 = (s32[256]{0:T(256)S(1)}, s32[256]{0:T(256)}, u32[]{:S(2)}) copy-start(s32[256]{0:T(256)} %param.16) | copy-start | bytes 3076
  7.3 101.5 %all-gather.7.cloned.1.call-start = ((), (), s32[]{:S(2)}) async-start(), calls=%async_computation.2 | async-start | bytes 2359296 | tf_op jit(solution)/shard_map/all_gather | solution.py:90
  22.4 5.1 %copy-start.3 = (bf16[256,2048]{1,0:T(8,128)(2,1)}, bf16[256,2048]{1,0:T(8,128)(2,1)S(1)}, u32[]{:S(2)}) copy-start(bf16[256,2048]{1,0:T(8,128)(2,1)S(1)} %fusion.13) | copy-start | bytes 3145732
  27.5 1.2 copy-start.1
  27.5 2.7 %copy-start.10 = (f32[4]{0:T(128)S(1)}, f32[4]{0:T(128)}, u32[]{:S(2)}) copy-start(f32[4]{0:T(128)} %param.24) | copy-start | bytes 52
  27.5 5.7 %copy-start.9 = (bf16[2048,4]{0,1:T(4,128)(2,1)S(1)}, bf16[2048,4]{0,1:T(4,128)(2,1)}, u32[]{:S(2)}) copy-start(bf16[2048,4]{0,1:T(4,128)(2,1)} %param.22) | copy-start | bytes 49156
  27.5 5.7 %copy-start.11 = (f32[4]{0:T(128)S(1)}, f32[4]{0:T(128)}, u32[]{:S(2)}) copy-start(f32[4]{0:T(128)} %param.23) | copy-start | bytes 52
  29.4 112.8 %all-gather.9.cloned.1.call-start = ((), (), s32[]{:S(2)}) async-start(), calls=%async_computation.4 | async-start | bytes 2359296 | tf_op jit(solution)/shard_map/all_gather | solution.py:91
  37.1 7.2 %copy-start.5 = (f32[1,4,2,128]{3,1,2,0:T(4,128)}, f32[1,4,2,128]{3,1,2,0:T(4,128)S(1)}, u32[]{:S(2)}) copy-start(f32[1,4,2,128]{3,1,2,0:T(4,128)S(1)} %copy.67) | copy-start | bytes 12292
  37.8 18.8 %collective-permute-start = (f32[4]{0:T(128)}, f32[4]{0:T(128)}, u32[]{:S(2)}, u32[]{:S(2)}) collective-permute-start(f32[4]{0:T(128)} %exp.49), channel_id=1, source_target_pairs={{14,0},{0,2},{2,4},{4,6},{6,8},{8,10},{10,12},{12,14},{15,1},{1,3}... | collective-permute-start | bytes 56 | tf_op jit(solution)/shard_map/ppermute | solution.py:17
  44.2 9.9 %copy-start.13 = (bf16[32,4,8,128]{3,2,1,0:T(8,128)(2,1)}, bf16[32,4,8,128]{3,2,1,0:T(8,128)(2,1)S(1)}, u32[]{:S(2)}) copy-start(bf16[32,4,8,128]{3,2,1,0:T(8,128)(2,1)S(1)} %fusion.43) | copy-start | bytes 786436
  45.2 28.8 %collective-permute-start.3 = (f32[4,128,64]{1,2,0:T(8,128)}, f32[4,128,64]{1,2,0:T(8,128)S(1)}, u32[]{:S(2)}, u32[]{:S(2)}) collective-permute-start(f32[4,128,64]{1,2,0:T(8,128)} %fusion.35), channel_id=1, source_target_pairs={{14,0},{0,2},{2,4},{4,6},{6,8},{8,10},{10,12},{12,14},{15,1},{1,3}... | collective-permute-start | bytes 393224 | tf_op jit(solution)/shard_map/ppermute | solution.py:17
  48.5 140.6 %reduce-scatter.2.cloned.1.call-start = ((), (), s32[]{:S(2)}) async-start(), calls=%async_computation.3 | async-start | bytes 3145728 | tf_op jit(solution)/shard_map/reduce_scatter | solution.py:202
  49.5 8.8 %collective-permute-start.8 = (f32[4]{0:T(128)}, f32[4]{0:T(128)}, u32[]{:S(2)}, u32[]{:S(2)}) collective-permute-start(f32[4]{0:T(128)} %exp.54), channel_id=1, source_target_pairs={{2,0},{4,2},{6,4},{8,6},{10,8},{12,10},{14,12},{0,14},{3,1},{5,3},... | collective-permute-start | bytes 56 | tf_op jit(solution)/shard_map/ppermute | solution.py:17
  53.8 19.7 %collective-permute-start.11 = (f32[4,128,64]{1,2,0:T(8,128)}, f32[4,128,64]{1,2,0:T(8,128)S(1)}, u32[]{:S(2)}, u32[]{:S(2)}) collective-permute-start(f32[4,128,64]{1,2,0:T(8,128)} %fusion.33), channel_id=1, source_target_pairs={{2,0},{4,2},{6,4},{8,6},{10,8},{12,10},{14,12},{0,14},{3,1},{5,3},... | collective-permute-start | bytes 393224 | tf_op jit(solution)/shard_map/ppermute | solution.py:17
  54.4 1.7 copy-start.14
  54.4 1.7 copy-start.15
  56.6 6.5 %collective-permute-start.1 = (f32[4]{0:T(128)}, f32[4]{0:T(128)S(1)}, u32[]{:S(2)}, u32[]{:S(2)}) collective-permute-start(f32[4]{0:T(128)} %collective-permute-done), channel_id=1, source_target_pairs={{14,0},{0,2},{2,4},{4,6},{6,8},{8,10},{10,12},{12,14},{15,1},{1,3}... | collective-permute-start | bytes 56 | tf_op jit(solution)/shard_map/ppermute | solution.py:17
  58.4 5.4 %collective-permute-start.9 = (f32[4]{0:T(128)}, f32[4]{0:T(128)S(1)}, u32[]{:S(2)}, u32[]{:S(2)}) collective-permute-start(f32[4]{0:T(128)} %collective-permute-done.8), channel_id=1, source_target_pairs={{2,0},{4,2},{6,4},{8,6},{10,8},{12,10},{14,12},{0,14},{3,1},{5,3},... | collective-permute-start | bytes 56 | tf_op jit(solution)/shard_map/ppermute | solution.py:17
  63.8 5.4 %collective-permute-start.2 = (f32[4]{0:T(128)S(1)}, f32[4]{0:T(128)S(1)}, u32[]{:S(2)}, u32[]{:S(2)}) collective-permute-start(f32[4]{0:T(128)S(1)} %mul.277), channel_id=1, source_target_pairs={{12,0},{14,2},{0,4},{2,6},{4,8},{6,10},{8,12},{10,14},{13,1},{15,3... | collective-permute-start | bytes 56 | tf_op jit(solution)/shard_map/ppermute | solution.py:17
  64.4 5.1 %collective-permute-start.10 = (f32[4]{0:T(128)S(1)}, f32[4]{0:T(128)S(1)}, u32[]{:S(2)}, u32[]{:S(2)}) collective-permute-start(f32[4]{0:T(128)S(1)} %mul.298), channel_id=1, source_target_pairs={{4,0},{6,2},{8,4},{10,6},{12,8},{14,10},{0,12},{2,14},{5,1},{7,3},... | collective-permute-start | bytes 56 | tf_op jit(solution)/shard_map/ppermute | solution.py:17
  69.1 4.5 %collective-permute-start.7 = (f32[4]{0:T(128)S(1)}, f32[4]{0:T(128)S(1)}, u32[]{:S(2)}, u32[]{:S(2)}) collective-permute-start(f32[4]{0:T(128)S(1)} %mul.278), channel_id=1, source_target_pairs={{8,0},{10,2},{12,4},{14,6},{0,8},{2,10},{4,12},{6,14},{9,1},{11,3}... | collective-permute-start | bytes 56 | tf_op jit(solution)/shard_map/ppermute | solution.py:17
  69.5 4.4 %collective-permute-start.15 = (f32[4]{0:T(128)S(1)}, f32[4]{0:T(128)S(1)}, u32[]{:S(2)}, u32[]{:S(2)}) collective-permute-start(f32[4]{0:T(128)S(1)} %mul.299), channel_id=1, source_target_pairs={{8,0},{10,2},{12,4},{14,6},{0,8},{2,10},{4,12},{6,14},{9,1},{11,3}... | collective-permute-start | bytes 56 | tf_op jit(solution)/shard_map/ppermute | solution.py:17
  73.6 5.9 %collective-permute-start.12 = (f32[4,128,64]{1,2,0:T(8,128)S(1)}, f32[4,128,64]{1,2,0:T(8,128)S(1)}, u32[]{:S(2)}, u32[]{:S(2)}) collective-permute-start(f32[4,128,64]{1,2,0:T(8,128)S(1)} %collective-permute-done.11), channel_id=1, source_target_pairs={{2,0},{4,2},{6,4},{8,6},{10,8},{12,10},{14,12},{0,14},{3,1},{5,3},... | collective-permute-start | bytes 393224 | tf_op jit(solution)/shard_map/ppermute | solution.py:17
  74.0 11.4 %collective-permute-start.4 = (f32[4,128,64]{1,2,0:T(8,128)S(1)}, f32[4,128,64]{1,2,0:T(8,128)S(1)}, u32[]{:S(2)}, u32[]{:S(2)}) collective-permute-start(f32[4,128,64]{1,2,0:T(8,128)S(1)} %collective-permute-done.3), channel_id=1, source_target_pairs={{14,0},{0,2},{2,4},{4,6},{6,8},{8,10},{10,12},{12,14},{15,1},{1,3}... | collective-permute-start | bytes 393224 | tf_op jit(solution)/shard_map/ppermute | solution.py:17
  80.2 6.4 %collective-permute-start.13 = (f32[4,128,64]{1,2,0:T(8,128)S(1)}, f32[4,128,64]{1,2,0:T(8,128)S(1)}, u32[]{:S(2)}, u32[]{:S(2)}) collective-permute-start(f32[4,128,64]{1,2,0:T(8,128)S(1)} %multiply_add_fusion.1), channel_id=1, source_target_pairs={{4,0},{6,2},{8,4},{10,6},{12,8},{14,10},{0,12},{2,14},{5,1},{7,3},... | collective-permute-start | bytes 393224 | tf_op jit(solution)/shard_map/ppermute | solution.py:17
  86.2 11.8 %collective-permute-start.5 = (f32[4,128,64]{1,2,0:T(8,128)S(1)}, f32[4,128,64]{1,2,0:T(8,128)S(1)}, u32[]{:S(2)}, u32[]{:S(2)}) collective-permute-start(f32[4,128,64]{1,2,0:T(8,128)S(1)} %multiply_add_fusion.3), channel_id=1, source_target_pairs={{12,0},{14,2},{0,4},{2,6},{4,8},{6,10},{8,12},{10,14},{13,1},{15,3... | collective-permute-start | bytes 393224 | tf_op jit(solution)/shard_map/ppermute | solution.py:17
  86.7 14.8 %collective-permute-start.14 = (f32[4,128,64]{1,2,0:T(8,128)S(1)}, f32[4,128,64]{1,2,0:T(8,128)S(1)}, u32[]{:S(2)}, u32[]{:S(2)}) collective-permute-start(f32[4,128,64]{1,2,0:T(8,128)S(1)} %multiply_add_fusion), channel_id=1, source_target_pairs={{8,0},{10,2},{12,4},{14,6},{0,8},{2,10},{4,12},{6,14},{9,1},{11,3}... | collective-permute-start | bytes 393224 | tf_op jit(solution)/shard_map/ppermute | solution.py:17
  98.0 10.2 %collective-permute-start.6 = (f32[4,128,64]{1,2,0:T(8,128)S(1)}, f32[4,128,64]{1,2,0:T(8,128)S(1)}, u32[]{:S(2)}, u32[]{:S(2)}) collective-permute-start(f32[4,128,64]{1,2,0:T(8,128)S(1)} %multiply_add_fusion.2), channel_id=1, source_target_pairs={{8,0},{10,2},{12,4},{14,6},{0,8},{2,10},{4,12},{6,14},{9,1},{11,3}... | collective-permute-start | bytes 393224 | tf_op jit(solution)/shard_map/ppermute | solution.py:17
  146.8 3.4 %copy-start.12 = (s32[4]{0:T(128)S(1)}, s32[4]{0:T(128)}, u32[]{:S(2)}) copy-start(s32[4]{0:T(128)} %iota_multiply_fusion) | copy-start | bytes 52
  150.1 28.6 %copy-start.7 = (f32[512]{0:T(512)S(1)}, f32[512]{0:T(512)}, u32[]{:S(2)}) copy-start(f32[512]{0:T(512)} %param.26) | copy-start | bytes 6148
  150.1 28.6 %copy-start.8 = (f32[512]{0:T(512)S(1)}, f32[512]{0:T(512)}, u32[]{:S(2)}) copy-start(f32[512]{0:T(512)} %param.25) | copy-start | bytes 6148
  181.1 8.0 %copy-start.2 = (bf16[256,1024]{1,0:T(8,128)(2,1)S(1)}, bf16[256,1024]{1,0:T(8,128)(2,1)}, u32[]{:S(2)}) copy-start(bf16[256,1024]{1,0:T(8,128)(2,1)} %param.15) | copy-start | bytes 1572868
Sparse Core Ops, SparseCore 0:
  8.9 11.7 all-gather.4
  29.6 61.0 all-gather.6
  92.7 49.5 all-gather.8
  181.2 7.7 reduce-scatter.1
where the time goes:
time: 199 us; the launch traced here: 198 us
  waiting for transfers between devices  61.6 us (31%)
  matrix products  41.7 us (21%)
  local copies, waits for them, and re-layouts  33.6 us (17%)
  starting transfers between devices  31 us (16%)
  other arithmetic  15.6 us (8%)
  between operations  14.1 us (7%)
    ppermute x16, starting transfers between devices, passed_along(): return lax.ppermute(block, axis, route)  30.9 us
    all_gather x1, waiting for transfers between devices, local(): value_piece = lax.all_gather(valueset, 'seq', axis=0, tiled=True)  24.4 us
    ppermute x16, waiting for transfers between devices, passed_along(): return lax.ppermute(block, axis, route)  24 us
    unnamed x38, local copies, waits for them, and re-layouts  18 us
    dot_general x4, matrix products, key_block(): jnp.einsum('epq,fpq->pef', query_tile_rows, key_fragment, preferred_eleme...  11.6 us
    dot_general x4, matrix products, key_block(): jnp.einsum('gfa,agn->fgn', weights.astype(jnp.bfloat16), value_piece, pre...  9.27 us
    reduce_scatter x1, waiting for transfers between devices, local(): lax.psum_scatter(partial_out, 'chan', scatter_dimension=1, tiled=True)  7.92 us
    lt x4, other arithmetic, key_block(): key_position < valid_limit  5.19 us
  transfers between devices with their start and end apart: 20, of which 13 were waited for; matrix products, arithmetic and copies ran while one was open for 21% of the time, Pallas kernels for 0%

commit v1 on v0

--- a/solution.py
+++ b/solution.py
@@ -3,6 +3,7 @@
 import jax.numpy as jnp
 from jax import lax
 from jax.sharding import PartitionSpec as P
+from jax.lax import all_gather
 
 HEAD_DIM = 128
 STATE = 64
@@ -61,6 +62,14 @@
     scan_gain,
     out_weight,
 ):
+
+    def leaf_attach(arr_in, vec, net_axis):
+        return jnp.split(
+            all_gather(jnp.concatenate([arr_in, vec], 1), axis_name=net_axis, axis=0, tiled=True),
+            [arr_in.shape[1]],
+            1,
+        )
+
     row_count = stream.shape[0]
     model_width = embedding.shape[1]
     head_count = step_weight.shape[1]
@@ -87,8 +96,7 @@
     empty_numer = jnp.zeros((row_count, head_count, HEAD_DIM), jnp.float32)
     empty_total = jnp.zeros((row_count, head_count), jnp.float32)
     carry_pair = (empty_numer, empty_total)
-    key_fragment = lax.all_gather(keyset, "seq", axis=0, tiled=True)
-    value_piece = lax.all_gather(valueset, "seq", axis=0, tiled=True)
+    key_fragment, value_piece = leaf_attach(keyset, valueset, "seq")
     piece_rows = key_fragment.shape[0]
     block_count = piece_rows // 512
 

time: 199 us -> 193 us (0.970)
  starting transfers between devices: 31 us -> 45.7 us
  waiting for transfers between devices: 61.6 us -> 48.8 us
  local copies, waits for them, and re-layouts: 33.6 us -> 29.7 us
  other arithmetic: 15.6 us -> 12 us
    all_gather x2 -> x1, waiting for transfers between devices: 24.4 us -> 4.54 us  [leaf_attach(): all_gather(jnp.concatenate([arr_in, vec], 1), axis_name=net_axis, axis=0,...]
    ppermute x16, starting transfers between devices: 30.9 us -> 45.6 us  [passed_along(): return lax.ppermute(block, axis, route)]
    split x0 -> x1, local copies, waits for them, and re-layouts: none -> 4.8 us  [leaf_attach(): jnp.split(all_gather(jnp.concatenate([arr_in, vec], 1), axis_name=net_axi...]
    unnamed x38 -> x29, local copies, waits for them, and re-layouts: 18 us -> 13.6 us
    reduce_scatter x1, waiting for transfers between devices: 7.92 us -> 11.7 us  [local(): lax.psum_scatter(partial_out, 'chan', scatter_dimension=1, tiled=True)]
    ppermute x16, waiting for transfers between devices: 24 us -> 27.3 us  [passed_along(): return lax.ppermute(block, axis, route)]
  transfers between devices with their start and end apart: 20 -> 19, of which waited for: 13 -> 10; matrix products, arithmetic and copies ran while one was open for 21% -> 13% of each run, Pallas kernels for 0% -> 0%
where the time goes in v1:
time: 193 us; the launch traced here: 192 us
  waiting for transfers between devices  48.8 us (25%)
  starting transfers between devices  45.7 us (24%)
  matrix products  41.4 us (21%)
  local copies, waits for them, and re-layouts  29.7 us (15%)
  between operations  14.1 us (7%)
  other arithmetic  12 us (6%)
    ppermute x16, starting transfers between devices, passed_along(): return lax.ppermute(block, axis, route)  45.6 us
    ppermute x16, waiting for transfers between devices, passed_along(): return lax.ppermute(block, axis, route)  27.3 us
    unnamed x29, local copies, waits for them, and re-layouts  13.6 us
    reduce_scatter x1, waiting for transfers between devices, local(): lax.psum_scatter(partial_out, 'chan', scatter_dimension=1, tiled=True)  11.7 us
    dot_general x4, matrix products, key_block(): jnp.einsum('epq,fpq->pef', query_tile_rows, key_fragment, preferred_eleme...  11.5 us
    dot_general x4, matrix products, key_block(): jnp.einsum('gfa,agn->fgn', weights.astype(jnp.bfloat16), value_piece, pre...  9.27 us
    lt x4, other arithmetic, key_block(): key_position < valid_limit  5.19 us
    dot_general x1, matrix products, local(): jnp.dot(hidden, attention_in.reshape(model_width, 3 * head_count * HEAD_D...  5.05 us
  transfers between devices with their start and end apart: 19, of which 10 were waited for; matrix products, arithmetic and copies ran while one was open for 13% of the time, Pallas kernels for 0%

profile of v1, /device:TPU:0, one launch (start us, length us, event | category | flops | bytes accessed | tf_op | source)
XLA Modules:
  0.0 191.9 jit_solution(12137568026409129019)
XLA Ops:
  7.3 8.8 %copy.26 = bf16[2048,3,512]{0,2,1:T(8,128)(2,1)} copy(bf16[2048,3,512]{2,0,1:T(8,128)(2,1)} %param.19) | data formatting | bytes 12582912 | tf_op args[4]
  16.2 4.5 %all-gather.3.cloned.1.call-done = bf16[256,2048]{1,0:T(8,128)(2,1)} async-done(((bf16[256,1024]{1,0:T(8,128)(2,1)}), bf16[256,2048]{1,0:T(8,128)(2,1)}) %all-gather.3.cloned.1.call-update) | async-done | bytes 1048592 | tf_op jit(solution)/shard_map/all_gather | solution.py:80
  20.7 1.7 fusion.13
  22.4 5.0 %fusion.17 = f32[256,3,4,128]{0,3,2,1:T(8,128)S(1)} fusion(bf16[3,4,128,2048]{3,2,1,0:T(8,128)(2,1)} %bitcast.162, bf16[256,2048]{1,0:T(8,128)(2,1)S(1)} %fusion.13), kind=kOutput, calls=%fused_computation.30 | convolution fusion | flops 1610612736 | bytes 8912896 | tf_op jit(solution)/shard_map/dot_general | solution.py:88
  29.7 1.6 add_multiply_fusion.1
  33.1 1.8 collective-permute-start
  35.0 1.9 multiply_convert_fusion.7
  36.9 2.9 %fusion.44 = bf16[32,4,8,128]{3,2,1,0:T(8,128)(2,1)S(1)} fusion(bf16[256,2048]{1,0:T(8,128)(2,1)} %copy-done.2, bf16[2048,512]{1,0:T(8,128)(2,1)} %param.20), kind=kOutput, calls=%fused_computation.75 | convolution fusion | flops 537526272 | bytes 3407872 | tf_op jit(solution)/shard_map/dot_general | solution.py:128
  40.8 1.5 collective-permute-start.3
  44.5 3.3 %collective-permute-start.8 = (f32[4]{0:T(128)S(1)}, f32[4]{0:T(128)S(1)}, u32[]{:S(2)}, u32[]{:S(2)}) collective-permute-start(f32[4]{0:T(128)S(1)} %exp.54), channel_id=1, source_target_pairs={{2,0},{4,2},{6,4},{8,6},{10,8},{12,10},{14,12},{0,14},{3,1},{5,3},... | collective-permute-start | bytes 56 | tf_op jit(solution)/shard_map/ppermute | solution.py:18
  47.8 1.3 fusion.34
  49.5 1.5 convolution_bitcast_fusion.2
  51.5 1.9 %collective-permute-start.1 = (f32[4]{0:T(128)S(1)}, f32[4]{0:T(128)S(1)}, u32[]{:S(2)}, u32[]{:S(2)}) collective-permute-start(f32[4]{0:T(128)S(1)} %collective-permute-done), channel_id=1, source_target_pairs={{14,0},{0,2},{2,4},{4,6},{6,8},{8,10},{10,12},{12,14},{15,1},{1,3}... | collective-permute-start | bytes 56 | tf_op jit(solution)/shard_map/ppermute | solution.py:18
  53.5 2.8 %collective-permute-start.9 = (f32[4]{0:T(128)S(1)}, f32[4]{0:T(128)S(1)}, u32[]{:S(2)}, u32[]{:S(2)}) collective-permute-start(f32[4]{0:T(128)S(1)} %collective-permute-done.8), channel_id=1, source_target_pairs={{2,0},{4,2},{6,4},{8,6},{10,8},{12,10},{14,12},{0,14},{3,1},{5,3},... | collective-permute-start | bytes 56 | tf_op jit(solution)/shard_map/ppermute | solution.py:18
  56.3 1.6 collective-permute-done.1
  57.9 3.8 %collective-permute-start.10 = (f32[4]{0:T(128)S(1)}, f32[4]{0:T(128)S(1)}, u32[]{:S(2)}, u32[]{:S(2)}) collective-permute-start(f32[4]{0:T(128)S(1)} %mul.298), channel_id=1, source_target_pairs={{4,0},{6,2},{8,4},{10,6},{12,8},{14,10},{0,12},{2,14},{5,1},{7,3},... | collective-permute-start | bytes 56 | tf_op jit(solution)/shard_map/ppermute | solution.py:18
  61.8 1.5 collective-permute-done.2
  63.3 2.9 %collective-permute-start.15 = (f32[4]{0:T(128)S(1)}, f32[4]{0:T(128)S(1)}, u32[]{:S(2)}, u32[]{:S(2)}) collective-permute-start(f32[4]{0:T(128)S(1)} %mul.299), channel_id=1, source_target_pairs={{8,0},{10,2},{12,4},{14,6},{0,8},{2,10},{4,12},{6,14},{9,1},{11,3}... | collective-permute-start | bytes 56 | tf_op jit(solution)/shard_map/ppermute | solution.py:18
  66.2 1.5 collective-permute-done.7
  68.1 1.7 collective-permute-start.4
  69.8 3.0 %collective-permute-done.12 = f32[4,128,64]{1,2,0:T(8,128)S(1)} collective-permute-done((f32[4,128,64]{1,2,0:T(8,128)S(1)}, f32[4,128,64]{1,2,0:T(8,128)S(1)}, u32[]{:S(2)}, u32[]{:S(2)}) %collective-permute-start.12) | collective-permute-done | bytes 131104 | tf_op jit(solution)/shard_map/ppermute | solution.py:18
  73.6 2.4 %collective-permute-done.4 = f32[4,128,64]{1,2,0:T(8,128)S(1)} collective-permute-done((f32[4,128,64]{1,2,0:T(8,128)S(1)}, f32[4,128,64]{1,2,0:T(8,128)S(1)}, u32[]{:S(2)}, u32[]{:S(2)}) %collective-permute-start.4) | collective-permute-done | bytes 131104 | tf_op jit(solution)/shard_map/ppermute | solution.py:18
  76.1 1.5 collective-permute-start.5
  77.7 5.0 %collective-permute-done.13 = f32[4,128,64]{1,2,0:T(8,128)S(1)} collective-permute-done((f32[4,128,64]{1,2,0:T(8,128)S(1)}, f32[4,128,64]{1,2,0:T(8,128)S(1)}, u32[]{:S(2)}, u32[]{:S(2)}) %collective-permute-start.13) | collective-permute-done | bytes 131104 | tf_op jit(solution)/shard_map/ppermute | solution.py:18
  82.8 8.3 %collective-permute-start.14 = (f32[4,128,64]{1,2,0:T(8,128)S(1)}, f32[4,128,64]{1,2,0:T(8,128)S(1)}, u32[]{:S(2)}, u32[]{:S(2)}) collective-permute-start(f32[4,128,64]{1,2,0:T(8,128)S(1)} %multiply_add_fusion), channel_id=1, source_target_pairs={{8,0},{10,2},{12,4},{14,6},{0,8},{2,10},{4,12},{6,14},{9,1},{11,3}... | collective-permute-start | bytes 393224 | tf_op jit(solution)/shard_map/ppermute | solution.py:18
  91.2 14.6 %collective-permute-start.6 = (f32[4,128,64]{1,2,0:T(8,128)S(1)}, f32[4,128,64]{1,2,0:T(8,128)S(1)}, u32[]{:S(2)}, u32[]{:S(2)}) collective-permute-start(f32[4,128,64]{1,2,0:T(8,128)S(1)} %multiply_add_fusion.2), channel_id=1, source_target_pairs={{8,0},{10,2},{12,4},{14,6},{0,8},{2,10},{4,12},{6,14},{9,1},{11,3}... | collective-permute-start | bytes 393224 | tf_op jit(solution)/shard_map/ppermute | solution.py:18
  106.3 12.2 %collective-permute-done.6 = f32[4,128,64]{1,2,0:T(8,128)S(1)} collective-permute-done((f32[4,128,64]{1,2,0:T(8,128)S(1)}, f32[4,128,64]{1,2,0:T(8,128)S(1)}, u32[]{:S(2)}, u32[]{:S(2)}) %collective-permute-start.6) | collective-permute-done | bytes 131104 | tf_op jit(solution)/shard_map/ppermute | solution.py:18
  119.1 4.5 %all-gather.5.cloned.1.call-done = bf16[2048,8,128]{0,2,1:T(8,128)(2,1)} async-done(((bf16[256,8,128]{0,2,1:T(8,128)(2,1)}), bf16[2048,8,128]{0,2,1:T(8,128)(2,1)}) %all-gather.5.cloned.1.call-update) | async-done | bytes 4194320 | tf_op jit(solution)/shard_map/all_gather | solution.py:68
  123.7 4.8 %fusion.78 = (bf16[2048,4,128]{0,2,1:T(8,128)(2,1)}, bf16[2048,4,128]{0,2,1:T(8,128)(2,1)}) fusion(bf16[2048,8,128]{0,2,1:T(8,128)(2,1)} %all-gather.5.cloned.1.call-done), kind=kLoop, calls=%fused_computation.140 | loop fusion | bytes 8388608 | tf_op jit(solution)/shard_map/split | solution.py:67
  128.5 4.5 %reshape.152 = bf16[4,512,4,128]{1,0,3,2:T(4,128)(2,1)} reshape(bf16[2048,4,128]{0,2,1:T(8,128)(2,1)} %get-tuple-element.113) | data formatting | bytes 4194304 | tf_op jit(solution)/shard_map/reshape | solution.py:120
  133.0 4.5 %copy.28 = bf16[4,512,4,128]{3,1,2,0:T(8,128)(2,1)} copy(bf16[4,512,4,128]{1,0,3,2:T(4,128)(2,1)} %reshape.152) | data formatting | bytes 4194304
  137.4 3.1 %copy.68 = bf16[4,16,4,8,512]{4,3,1,0,2:T(8,128)(2,1)} copy(bf16[4,16,4,8,512]{4,3,2,1,0:T(8,128)(2,1)} %bitcast.161) | data formatting | bytes 4194304 | tf_op jit(solution)/shard_map/reshape | solution.py:121
  140.6 28.4 %while.13 = (s32[]{:T(128)}, f32[256,4,128]{0,2,1:T(8,128)S(1)}, f32[256,4]{0,1:T(4,128)S(1)}, bf16[4,512,4,128]{1,3,2,0:T(8,128)(2,1)}, s32[4]{0:T(128)S(1)}, /...) while((s32[]{:T(128)}, f32[256,4,128]{0,2,1:T(8,128)S(1)}, ...), condition=%wide.region_4.5_spmd.clone, body=%wide.region_2.4_spmd.clone.sunk | while | flops 271845376 | bytes 6572676 | solution.py:116
  141.2 1.3 add_compare_fusion.2
  142.5 2.9 %bitcast_reduce_fusion.2 = (f32[4,256]{1,0:T(4,128)S(1)}, f32[4,512,256]{2,1,0:T(8,128)}) fusion(pred[512]{0:T(512)(128)(4,1)S(1)} %add_compare_fusion.2, bf16[256,4,128]{2,0,1:T(8,128)(2,1)S(1)} %get-tuple-element.211, bf16[4,512,4,128]{3,1,2,0:T(8,128)(2,1)} %get-tuple-element.210, s32[]{:T(128)} %get-tuple-element.194), kind=kOutput, calls=%fused_computation.clone.1 | convolution fusion | flops 135789568 | bytes 2888704 | tf_op jit(solution)/shard_map/while/body/eval_jaxpr/epq,fpq->pef/dot_general | solution.py:34
  145.3 2.3 %fusion.96 = f32[256,4,128]{0,2,1:T(8,128)S(1)} fusion(f32[4,512,256]{2,1,0:T(8,128)} %get-tuple-element.182, pred[512]{0:T(512)(128)(4,1)S(1)} %add_compare_fusion.2, f32[256,4,128]{0,2,1:T(8,128)S(1)} %get-tuple-element.195, bf16[4,512,4,128]{1,3,2,0:T(8,128)(2,1)} %get-tuple-element.207, s32[]{:T(128)} %get-tuple-element.194, pred[]{:T(512)S(6)} %compare.3), kind=kOutput, calls=%fused_computation.4.clone.1 | convolution fusion | flops 136052736 | bytes 3671041 | tf_op jit(solution)/shard_map/while/body/eval_jaxpr/gfa,agn->fgn/dot_general | solution.py:41
  148.3 1.3 add_compare_fusion.2
  149.6 2.9 %bitcast_reduce_fusion.2 = (f32[4,256]{1,0:T(4,128)S(1)}, f32[4,512,256]{2,1,0:T(8,128)}) fusion(pred[512]{0:T(512)(128)(4,1)S(1)} %add_compare_fusion.2, bf16[256,4,128]{2,0,1:T(8,128)(2,1)S(1)} %get-tuple-element.211, bf16[4,512,4,128]{3,1,2,0:T(8,128)(2,1)} %get-tuple-element.210, s32[]{:T(128)} %get-tuple-element.194), kind=kOutput, calls=%fused_computation.clone.1 | convolution fusion | flops 135789568 | bytes 2888704 | tf_op jit(solution)/shard_map/while/body/eval_jaxpr/epq,fpq->pef/dot_general | solution.py:34
  152.5 2.3 %fusion.96 = f32[256,4,128]{0,2,1:T(8,128)S(1)} fusion(f32[4,512,256]{2,1,0:T(8,128)} %get-tuple-element.182, pred[512]{0:T(512)(128)(4,1)S(1)} %add_compare_fusion.2, f32[256,4,128]{0,2,1:T(8,128)S(1)} %get-tuple-element.195, bf16[4,512,4,128]{1,3,2,0:T(8,128)(2,1)} %get-tuple-element.207, s32[]{:T(128)} %get-tuple-element.194, pred[]{:T(512)S(6)} %compare.3), kind=kOutput, calls=%fused_computation.4.clone.1 | convolution fusion | flops 136052736 | bytes 3671041 | tf_op jit(solution)/shard_map/while/body/eval_jaxpr/gfa,agn->fgn/dot_general | solution.py:41
  155.4 1.3 add_compare_fusion.2
  156.7 2.9 %bitcast_reduce_fusion.2 = (f32[4,256]{1,0:T(4,128)S(1)}, f32[4,512,256]{2,1,0:T(8,128)}) fusion(pred[512]{0:T(512)(128)(4,1)S(1)} %add_compare_fusion.2, bf16[256,4,128]{2,0,1:T(8,128)(2,1)S(1)} %get-tuple-element.211, bf16[4,512,4,128]{3,1,2,0:T(8,128)(2,1)} %get-tuple-element.210, s32[]{:T(128)} %get-tuple-element.194), kind=kOutput, calls=%fused_computation.clone.1 | convolution fusion | flops 135789568 | bytes 2888704 | tf_op jit(solution)/shard_map/while/body/eval_jaxpr/epq,fpq->pef/dot_general | solution.py:34
  159.6 2.3 %fusion.96 = f32[256,4,128]{0,2,1:T(8,128)S(1)} fusion(f32[4,512,256]{2,1,0:T(8,128)} %get-tuple-element.182, pred[512]{0:T(512)(128)(4,1)S(1)} %add_compare_fusion.2, f32[256,4,128]{0,2,1:T(8,128)S(1)} %get-tuple-element.195, bf16[4,512,4,128]{1,3,2,0:T(8,128)(2,1)} %get-tuple-element.207, s32[]{:T(128)} %get-tuple-element.194, pred[]{:T(512)S(6)} %compare.3), kind=kOutput, calls=%fused_computation.4.clone.1 | convolution fusion | flops 136052736 | bytes 3671041 | tf_op jit(solution)/shard_map/while/body/eval_jaxpr/gfa,agn->fgn/dot_general | solution.py:41
  162.5 1.3 add_compare_fusion.2
  163.8 2.9 %bitcast_reduce_fusion.2 = (f32[4,256]{1,0:T(4,128)S(1)}, f32[4,512,256]{2,1,0:T(8,128)}) fusion(pred[512]{0:T(512)(128)(4,1)S(1)} %add_compare_fusion.2, bf16[256,4,128]{2,0,1:T(8,128)(2,1)S(1)} %get-tuple-element.211, bf16[4,512,4,128]{3,1,2,0:T(8,128)(2,1)} %get-tuple-element.210, s32[]{:T(128)} %get-tuple-element.194), kind=kOutput, calls=%fused_computation.clone.1 | convolution fusion | flops 135789568 | bytes 2888704 | tf_op jit(solution)/shard_map/while/body/eval_jaxpr/epq,fpq->pef/dot_general | solution.py:34
  166.7 2.3 %fusion.96 = f32[256,4,128]{0,2,1:T(8,128)S(1)} fusion(f32[4,512,256]{2,1,0:T(8,128)} %get-tuple-element.182, pred[512]{0:T(512)(128)(4,1)S(1)} %add_compare_fusion.2, f32[256,4,128]{0,2,1:T(8,128)S(1)} %get-tuple-element.195, bf16[4,512,4,128]{1,3,2,0:T(8,128)(2,1)} %get-tuple-element.207, s32[]{:T(128)} %get-tuple-element.194, pred[]{:T(512)S(6)} %compare.3), kind=kOutput, calls=%fused_computation.4.clone.1 | convolution fusion | flops 136052736 | bytes 3671041 | tf_op jit(solution)/shard_map/while/body/eval_jaxpr/gfa,agn->fgn/dot_general | solution.py:41
  169.4 2.1 %fusion.79 = f32[256,2048]{1,0:T(8,128)} fusion(bf16[256,512]{0,1:T(8,128)(2,1)S(1)} %bitcast.163, bf16[512,2048]{1,0:T(8,128)(2,1)S(1)} %copy-done), kind=kOutput, calls=%fused_computation.141 | convolution fusion | flops 536870912 | bytes 4456448 | tf_op jit(solution)/shard_map/dot_general | solution.py:209
  171.5 11.7 %reduce-scatter.2.cloned.1.call-done = f32[256,1024]{1,0:T(8,128)} async-done(((f32[256,2048]{1,0:T(8,128)}), f32[256,1024]{1,0:T(8,128)}) %reduce-scatter.2.cloned.1.call-update) | async-done | bytes 1048592 | tf_op jit(solution)/shard_map/reduce_scatter | solution.py:210
  183.2 2.2 %add_convert_fusion = bf16[256,1024]{1,0:T(8,128)(2,1)} fusion(f32[256,1024]{1,0:T(8,128)} %reduce-scatter.2.cloned.1.call-done, bf16[256,1024]{1,0:T(8,128)(2,1)S(1)} %copy-done.1), kind=kLoop, calls=%fused_computation.32 | loop fusion | flops 786432 | bytes 2097152 | tf_op jit(solution)/shard_map/convert_element_type | solution.py:211
  (111 shorter events, 13.5 us)
Async XLA Ops:
  6.5 162.8 %copy-start = (bf16[512,2048]{1,0:T(8,128)(2,1)S(1)}, bf16[512,2048]{1,0:T(8,128)(2,1)}, u32[]{:S(2)}) copy-start(bf16[512,2048]{1,0:T(8,128)(2,1)} %param.27) | copy-start | bytes 6291460
  6.5 14.1 %all-gather.3.cloned.1.call-start = ((), (), s32[]{:S(2)}) async-start(), calls=%async_computation.1 | async-start | bytes 1572864 | tf_op jit(solution)/shard_map/all_gather | solution.py:80
  7.3 13.4 %copy-start.3 = (bf16[16,2048]{1,0:T(8,128)(2,1)S(1)}, bf16[16,2048]{1,0:T(8,128)(2,1)}, u32[]{:S(2)}) copy-start(bf16[16,2048]{1,0:T(8,128)(2,1)} %param.18) | copy-start | bytes 196612
  7.3 13.4 %copy-start.4 = (s32[256]{0:T(256)S(1)}, s32[256]{0:T(256)}, u32[]{:S(2)}) copy-start(s32[256]{0:T(256)} %param.16) | copy-start | bytes 3076
  7.3 116.4 %all-gather.5.cloned.1.call-start = ((), (), s32[]{:S(2)}) async-start(), calls=%async_computation.2 | async-start | bytes 4718592 | tf_op jit(solution)/shard_map/all_gather | solution.py:68
  22.4 5.1 %copy-start.2 = (bf16[256,2048]{1,0:T(8,128)(2,1)}, bf16[256,2048]{1,0:T(8,128)(2,1)S(1)}, u32[]{:S(2)}) copy-start(bf16[256,2048]{1,0:T(8,128)(2,1)S(1)} %fusion.13) | copy-start | bytes 3145732
  27.5 1.8 copy-start.8
  27.6 2.1 %copy-start.7 = (bf16[2048,4]{0,1:T(4,128)(2,1)S(1)}, bf16[2048,4]{0,1:T(4,128)(2,1)}, u32[]{:S(2)}) copy-start(bf16[2048,4]{0,1:T(4,128)(2,1)} %param.22) | copy-start | bytes 49156
  27.6 2.1 %copy-start.9 = (f32[4]{0:T(128)S(1)}, f32[4]{0:T(128)}, u32[]{:S(2)}) copy-start(f32[4]{0:T(128)} %param.23) | copy-start | bytes 52
  28.6 154.5 %reduce-scatter.2.cloned.1.call-start = ((), (), s32[]{:S(2)}) async-start(), calls=%async_computation.3 | async-start | bytes 3145728 | tf_op jit(solution)/shard_map/reduce_scatter | solution.py:210
  33.1 18.4 %collective-permute-start = (f32[4]{0:T(128)S(1)}, f32[4]{0:T(128)S(1)}, u32[]{:S(2)}, u32[]{:S(2)}) collective-permute-start(f32[4]{0:T(128)S(1)} %exp.49), channel_id=1, source_target_pairs={{14,0},{0,2},{2,4},{4,6},{6,8},{8,10},{10,12},{12,14},{15,1},{1,3}... | collective-permute-start | bytes 56 | tf_op jit(solution)/shard_map/ppermute | solution.py:18
  39.8 2.5 %copy-start.10 = (bf16[32,4,8,128]{3,2,1,0:T(8,128)(2,1)}, bf16[32,4,8,128]{3,2,1,0:T(8,128)(2,1)S(1)}, u32[]{:S(2)}) copy-start(bf16[32,4,8,128]{3,2,1,0:T(8,128)(2,1)S(1)} %fusion.44) | copy-start | bytes 786436
  40.8 27.3 %collective-permute-start.3 = (f32[4,128,64]{1,2,0:T(8,128)}, f32[4,128,64]{1,2,0:T(8,128)S(1)}, u32[]{:S(2)}, u32[]{:S(2)}) collective-permute-start(f32[4,128,64]{1,2,0:T(8,128)} %fusion.36), channel_id=1, source_target_pairs={{14,0},{0,2},{2,4},{4,6},{6,8},{8,10},{10,12},{12,14},{15,1},{1,3}... | collective-permute-start | bytes 393224 | tf_op jit(solution)/shard_map/ppermute | solution.py:18
  44.3 6.7 %copy-start.11 = (bf16[32,4,8,128]{3,2,1,0:T(8,128)(2,1)S(1)}, bf16[32,4,8,128]{3,2,1,0:T(8,128)(2,1)}, u32[]{:S(2)}) copy-start(bf16[32,4,8,128]{3,2,1,0:T(8,128)(2,1)} %copy-done.10) | copy-start | bytes 786436
  44.5 9.0 %collective-permute-start.8 = (f32[4]{0:T(128)S(1)}, f32[4]{0:T(128)S(1)}, u32[]{:S(2)}, u32[]{:S(2)}) collective-permute-start(f32[4]{0:T(128)S(1)} %exp.54), channel_id=1, source_target_pairs={{2,0},{4,2},{6,4},{8,6},{10,8},{12,10},{14,12},{0,14},{3,1},{5,3},... | collective-permute-start | bytes 56 | tf_op jit(solution)/shard_map/ppermute | solution.py:18
  49.1 18.6 %collective-permute-start.11 = (f32[4,128,64]{1,2,0:T(8,128)S(1)}, f32[4,128,64]{1,2,0:T(8,128)S(1)}, u32[]{:S(2)}, u32[]{:S(2)}) collective-permute-start(f32[4,128,64]{1,2,0:T(8,128)S(1)} %fusion.34), channel_id=1, source_target_pairs={{2,0},{4,2},{6,4},{8,6},{10,8},{12,10},{14,12},{0,14},{3,1},{5,3},... | collective-permute-start | bytes 393224 | tf_op jit(solution)/shard_map/ppermute | solution.py:18
  51.5 6.4 %collective-permute-start.1 = (f32[4]{0:T(128)S(1)}, f32[4]{0:T(128)S(1)}, u32[]{:S(2)}, u32[]{:S(2)}) collective-permute-start(f32[4]{0:T(128)S(1)} %collective-permute-done), channel_id=1, source_target_pairs={{14,0},{0,2},{2,4},{4,6},{6,8},{8,10},{10,12},{12,14},{15,1},{1,3}... | collective-permute-start | bytes 56 | tf_op jit(solution)/shard_map/ppermute | solution.py:18
  53.5 4.5 %collective-permute-start.9 = (f32[4]{0:T(128)S(1)}, f32[4]{0:T(128)S(1)}, u32[]{:S(2)}, u32[]{:S(2)}) collective-permute-start(f32[4]{0:T(128)S(1)} %collective-permute-done.8), channel_id=1, source_target_pairs={{2,0},{4,2},{6,4},{8,6},{10,8},{12,10},{14,12},{0,14},{3,1},{5,3},... | collective-permute-start | bytes 56 | tf_op jit(solution)/shard_map/ppermute | solution.py:18
  57.9 5.3 %collective-permute-start.2 = (f32[4]{0:T(128)S(1)}, f32[4]{0:T(128)S(1)}, u32[]{:S(2)}, u32[]{:S(2)}) collective-permute-start(f32[4]{0:T(128)S(1)} %mul.277), channel_id=1, source_target_pairs={{12,0},{14,2},{0,4},{2,6},{4,8},{6,10},{8,12},{10,14},{13,1},{15,3... | collective-permute-start | bytes 56 | tf_op jit(solution)/shard_map/ppermute | solution.py:18
  57.9 5.3 %collective-permute-start.10 = (f32[4]{0:T(128)S(1)}, f32[4]{0:T(128)S(1)}, u32[]{:S(2)}, u32[]{:S(2)}) collective-permute-start(f32[4]{0:T(128)S(1)} %mul.298), channel_id=1, source_target_pairs={{4,0},{6,2},{8,4},{10,6},{12,8},{14,10},{0,12},{2,14},{5,1},{7,3},... | collective-permute-start | bytes 56 | tf_op jit(solution)/shard_map/ppermute | solution.py:18
  63.3 4.4 %collective-permute-start.7 = (f32[4]{0:T(128)S(1)}, f32[4]{0:T(128)S(1)}, u32[]{:S(2)}, u32[]{:S(2)}) collective-permute-start(f32[4]{0:T(128)S(1)} %mul.278), channel_id=1, source_target_pairs={{8,0},{10,2},{12,4},{14,6},{0,8},{2,10},{4,12},{6,14},{9,1},{11,3}... | collective-permute-start | bytes 56 | tf_op jit(solution)/shard_map/ppermute | solution.py:18
  63.3 4.8 %collective-permute-start.15 = (f32[4]{0:T(128)S(1)}, f32[4]{0:T(128)S(1)}, u32[]{:S(2)}, u32[]{:S(2)}) collective-permute-start(f32[4]{0:T(128)S(1)} %mul.299), channel_id=1, source_target_pairs={{8,0},{10,2},{12,4},{14,6},{0,8},{2,10},{4,12},{6,14},{9,1},{11,3}... | collective-permute-start | bytes 56 | tf_op jit(solution)/shard_map/ppermute | solution.py:18
  67.7 5.1 %collective-permute-start.12 = (f32[4,128,64]{1,2,0:T(8,128)S(1)}, f32[4,128,64]{1,2,0:T(8,128)S(1)}, u32[]{:S(2)}, u32[]{:S(2)}) collective-permute-start(f32[4,128,64]{1,2,0:T(8,128)S(1)} %collective-permute-done.11), channel_id=1, source_target_pairs={{2,0},{4,2},{6,4},{8,6},{10,8},{12,10},{14,12},{0,14},{3,1},{5,3},... | collective-permute-start | bytes 393224 | tf_op jit(solution)/shard_map/ppermute | solution.py:18
  68.1 7.9 %collective-permute-start.4 = (f32[4,128,64]{1,2,0:T(8,128)S(1)}, f32[4,128,64]{1,2,0:T(8,128)S(1)}, u32[]{:S(2)}, u32[]{:S(2)}) collective-permute-start(f32[4,128,64]{1,2,0:T(8,128)S(1)} %collective-permute-done.3), channel_id=1, source_target_pairs={{14,0},{0,2},{2,4},{4,6},{6,8},{8,10},{10,12},{12,14},{15,1},{1,3}... | collective-permute-start | bytes 393224 | tf_op jit(solution)/shard_map/ppermute | solution.py:18
  72.9 9.8 %collective-permute-start.13 = (f32[4,128,64]{1,2,0:T(8,128)S(1)}, f32[4,128,64]{1,2,0:T(8,128)S(1)}, u32[]{:S(2)}, u32[]{:S(2)}) collective-permute-start(f32[4,128,64]{1,2,0:T(8,128)S(1)} %multiply_add_fusion.1), channel_id=1, source_target_pairs={{4,0},{6,2},{8,4},{10,6},{12,8},{14,10},{0,12},{2,14},{5,1},{7,3},... | collective-permute-start | bytes 393224 | tf_op jit(solution)/shard_map/ppermute | solution.py:18
  76.1 15.0 %collective-permute-start.5 = (f32[4,128,64]{1,2,0:T(8,128)S(1)}, f32[4,128,64]{1,2,0:T(8,128)S(1)}, u32[]{:S(2)}, u32[]{:S(2)}) collective-permute-start(f32[4,128,64]{1,2,0:T(8,128)S(1)} %multiply_add_fusion.3), channel_id=1, source_target_pairs={{12,0},{14,2},{0,4},{2,6},{4,8},{6,10},{8,12},{10,14},{13,1},{15,3... | collective-permute-start | bytes 393224 | tf_op jit(solution)/shard_map/ppermute | solution.py:18
  82.8 23.0 %collective-permute-start.14 = (f32[4,128,64]{1,2,0:T(8,128)S(1)}, f32[4,128,64]{1,2,0:T(8,128)S(1)}, u32[]{:S(2)}, u32[]{:S(2)}) collective-permute-start(f32[4,128,64]{1,2,0:T(8,128)S(1)} %multiply_add_fusion), channel_id=1, source_target_pairs={{8,0},{10,2},{12,4},{14,6},{0,8},{2,10},{4,12},{6,14},{9,1},{11,3}... | collective-permute-start | bytes 393224 | tf_op jit(solution)/shard_map/ppermute | solution.py:18
  91.2 27.4 %collective-permute-start.6 = (f32[4,128,64]{1,2,0:T(8,128)S(1)}, f32[4,128,64]{1,2,0:T(8,128)S(1)}, u32[]{:S(2)}, u32[]{:S(2)}) collective-permute-start(f32[4,128,64]{1,2,0:T(8,128)S(1)} %multiply_add_fusion.2), channel_id=1, source_target_pairs={{8,0},{10,2},{12,4},{14,6},{0,8},{2,10},{4,12},{6,14},{9,1},{11,3}... | collective-permute-start | bytes 393224 | tf_op jit(solution)/shard_map/ppermute | solution.py:18
  140.6 28.5 %copy-start.5 = (f32[512]{0:T(512)S(1)}, f32[512]{0:T(512)}, u32[]{:S(2)}) copy-start(f32[512]{0:T(512)} %param.26) | copy-start | bytes 6148
  140.6 28.5 %copy-start.6 = (f32[512]{0:T(512)S(1)}, f32[512]{0:T(512)}, u32[]{:S(2)}) copy-start(f32[512]{0:T(512)} %param.25) | copy-start | bytes 6148
  171.4 11.7 %copy-start.1 = (bf16[256,1024]{1,0:T(8,128)(2,1)S(1)}, bf16[256,1024]{1,0:T(8,128)(2,1)}, u32[]{:S(2)}) copy-start(bf16[256,1024]{1,0:T(8,128)(2,1)} %param.15) | copy-start | bytes 1572868
Sparse Core Ops, SparseCore 0:
  8.9 11.7 all-gather.2
  28.7 94.8 all-gather.4
  171.6 11.5 reduce-scatter.1
